TPU v7x, 32 devices: a whole 2x2x4 slice. The times are simulated.
32 devices in a mesh: section: 4 (over x, core), mp: 8 (over z, y).
Axes of the slice: x: 2, y: 2, z: 4, core: 2. Of those that a mesh axis runs over, the one named last changes fastest.
Arguments:
- activations: bfloat16 [4, 64, 4096], P('section', 'mp'), may hold values from -24 to 24
- enc_weight: bfloat16 [4, 4096, 4096], P('section', None, 'mp'), may hold values from -0.046875 to 0.046875
- enc_bias: float32 [4096], P('mp'), may hold values from -4 to 4
- dec_weight: bfloat16 [4096, 4, 4096], P('mp', 'section'), may hold values from -2.1875 to 2.1875
- dec_bias: float32 [4, 4096], P('section'), may hold values from -3 to 3
Outputs:
- loss: float32 [], replicated
- grad_dec: bfloat16 [4096, 4, 4096], P('mp', 'section')
- grad_bias: float32 [4, 4096], P('section', 'mp')
All inputs are finite; a program needn't handle non-finite values.
Results may differ from a plain program's by a relative error of at most 0.009.
Values may be sent and summed in bfloat16 or wider, within the bound.
A program may use at most 64 MiB of HBM per device.

v0:
```python
import jax
import jax.numpy as jnp
from jax import lax
from jax.sharding import PartitionSpec as P

penalty_weight = 2.0


def local(activations, enc_weight, enc_bias, dec_weight, dec_bias):
    all_rows = lax.all_gather(activations[0], "mp", axis=0, tiled=True)
    token_count = all_rows.shape[0]
    partial_value = jnp.dot(all_rows, enc_weight[0], preferred_element_type=jnp.float32)
    w_dec = dec_weight[:, 0, :]
    layer_norm = jnp.sqrt(jnp.sum(jnp.square(w_dec.astype(jnp.float32)), axis=1) + 1e-06)
    pre_sum, norm_total = (
        lax.psum(partial_value.astype(jnp.bfloat16), "section").astype(jnp.float32),
        lax.psum(layer_norm.astype(jnp.bfloat16), "section").astype(jnp.float32),
    )
    latents = jnp.maximum(pre_sum + enc_bias[None, :], 0.0).astype(jnp.bfloat16)
    latent_float = latents.astype(jnp.float32)
    latent_sum = jnp.sum(latent_float, axis=0)
    penalty_part = penalty_weight / token_count * jnp.sum(latent_float * norm_total[None, :])
    penalty_part = jnp.where(lax.axis_index("section") == 0, penalty_part, 0.0)
    coef = penalty_weight * latent_sum / token_count / layer_norm
    col_width = w_dec.shape[1] // lax.axis_size("mp")
    first_col = lax.axis_index("mp") * col_width
    recon_t = lax.psum_scatter(
        lax.dot_general(
            w_dec, latents, (((0,), (1,)), ((), ())), preferred_element_type=jnp.float32
        ),
        "mp",
        scatter_dimension=0,
        tiled=True,
    )
    bias_cols = lax.dynamic_slice_in_dim(dec_bias[0], first_col, col_width, 0)
    x_cols = lax.dynamic_slice_in_dim(all_rows, first_col, col_width, 1)
    error_cols = recon_t + bias_cols[:, None] - x_cols.T.astype(jnp.float32)
    square_sum = jnp.sum(error_cols * error_cols)
    scaled = 2.0 * error_cols / token_count
    grad_rec_t = scaled.astype(jnp.bfloat16)
    grad_bias = jnp.sum(scaled, axis=1)[None, :]
    grad_sum = lax.dot_general(
        latents,
        lax.all_gather(grad_rec_t, "mp", axis=0, tiled=True),
        (((0,), (1,)), ((), ())),
        preferred_element_type=jnp.float32,
    )
    grad_dec = (grad_sum + coef[:, None] * w_dec.astype(jnp.float32)).astype(jnp.bfloat16)[
        :, None, :
    ]
    loss = lax.psum(square_sum / token_count + penalty_part, ("section", "mp"))
    return (loss, grad_dec, grad_bias)


def solution(mesh):
    in_specs = (
        P("section", "mp", None),
        P("section", None, "mp"),
        P("mp"),
        P("mp", "section", None),
        P("section", None),
    )
    out_specs = (P(), P("mp", "section", None), P("section", "mp"))
    return jax.shard_map(local, mesh=mesh, in_specs=in_specs, out_specs=out_specs, check_vma=False)
```

profile of v0, /device:TPU:0, one launch (start us, length us, event | category | flops | bytes accessed | tf_op | source)
XLA Modules:
  0.0 231.0 jit_solution(3103381486748929811)
XLA Ops:
  7.2 0.0 copy-start
  7.2 0.0 copy-start.2
  7.2 0.0 all-reduce.2.cloned.1.call-start
  7.2 33.2 %all-gather = bf16[1,64,4096]{2,1,0:T(8,128)(2,1)S(1)} all-gather(bf16[1,8,4096]{2,1,0:T(8,128)(2,1)} %param.5), channel_id=2, replica_groups=mesh['section'=4,'mp'=8] {'mp'}, dimensions={1}, use_global_device_ids=true | all-gather | bytes 589824 | tf_op jit(solution)/shard_map/all_gather | solution.py:10
  40.5 3.7 %fusion.7 = bf16[64,512]{1,0:T(8,128)(2,1)} fusion(bf16[1,4096,512]{2,1,0:T(8,128)(2,1)} %param.6, bf16[1,64,4096]{2,1,0:T(8,128)(2,1)S(1)} %all-gather), kind=kOutput, calls=%fused_computation.10 | convolution fusion | flops 268468224 | bytes 4784128 | tf_op jit(solution)/shard_map/dot_general | solution.py:12
  44.1 0.0 all-reduce.2.cloned.1.call-update
  44.2 0.0 reduce-scatter.2.cloned.1.call-start
  44.2 32.7 %all-reduce.2.cloned.1.call-done = bf16[64,512]{1,0:T(8,128)(2,1)} async-done(((bf16[64,512]{1,0:T(8,128)(2,1)}), bf16[64,512]{1,0:T(8,128)(2,1)}) %all-reduce.2.cloned.1.call-update) | async-done | bytes 65552 | tf_op jit(solution)/shard_map/psum | solution.py:16
  76.9 0.0 copy-done.2
  76.9 0.0 copy-start.1
  76.9 4.1 %convolution_bitcast_fusion = f32[4096,64]{0,1:T(8,128)} fusion(bf16[512,1,4096]{2,0,1:T(8,128)(2,1)} %param.8, bf16[64,512]{1,0:T(8,128)(2,1)} %all-reduce.2.cloned.1.call-done, f32[512]{0:T(512)S(1)} %copy-done.2), kind=kOutput, calls=%fused_computation.6 | convolution fusion | flops 268566528 | bytes 5310464 | tf_op jit(solution)/shard_map/dot_general | solution.py:28
  81.0 0.0 reduce-scatter.2.cloned.1.call-update
  81.1 3.1 %fusion = f32[512]{0:T(512)S(1)} fusion(bf16[512,1,4096]{2,0,1:T(8,128)(2,1)} %param.8), kind=kLoop, calls=%fused_computation.2 | loop fusion | flops 6290944 | bytes 4196352 | tf_op jit(solution)/shard_map/reduce_sum | solution.py:14
  84.1 5.8 %psum.22 = bf16[512]{0:T(512)(128)(2,1)S(1)} all-reduce(bf16[512]{0:T(512)(128)(2,1)S(1)} %sqrt_convert_fusion), channel_id=1, replica_groups=mesh['section'=4,'mp'=8] {'section'}, use_global_device_ids=true, to_apply=%region_4.0 | all-reduce | flops 512 | bytes 2048 | tf_op jit(solution)/shard_map/psum | solution.py:17
  89.9 0.0 copy-done
  89.9 0.0 copy-done.1
  89.9 0.6 convert_reduce_fusion
  91.2 54.2 %reduce-scatter.2.cloned.1.call-done = f32[512,64]{0,1:T(8,128)} async-done(((f32[4096,64]{0,1:T(8,128)}), f32[512,64]{0,1:T(8,128)}) %reduce-scatter.2.cloned.1.call-update) | async-done | bytes 131088 | tf_op jit(solution)/shard_map/reduce_scatter | solution.py:27
  145.5 1.5 multiply_reduce_fusion.1
  147.7 39.8 %psum.23 = f32[]{:T(128)} all-reduce(f32[]{:T(128)S(6)} %add.54), channel_id=1, replica_groups=mesh['section'=4,'mp'=8] {'section','mp'}, use_global_device_ids=true, to_apply=%region_6.7 | all-reduce | flops 1 | bytes 8 | tf_op jit(solution)/shard_map/psum | solution.py:51
  187.5 31.2 %all_gather.7 = bf16[4096,64]{0,1:T(8,128)(2,1)S(1)} all-gather(bf16[512,64]{0,1:T(8,128)(2,1)S(1)} %get-tuple-element.7), channel_id=1, replica_groups=mesh['section'=4,'mp'=8] {'mp'}, dimensions={0}, use_global_device_ids=true | all-gather | bytes 589824 | tf_op jit(solution)/shard_map/all_gather | solution.py:44
  218.7 5.5 %fusion.3 = bf16[512,1,4096]{2,0,1:T(8,128)(2,1)} fusion(bf16[4096,64]{0,1:T(8,128)(2,1)S(1)} %all_gather.7, bf16[512,1,4096]{2,0,1:T(8,128)(2,1)} %param.8, f32[512]{0:T(512)S(1)} %rsqrt_multiply_fusion, bf16[64,512]{1,0:T(8,128)(2,1)S(1)} %copy-done.1, f32[512]{0:T(512)S(1)} %copy-done.2), kind=kOutput, calls=%fused_computation.5 | convolution fusion | flops 276955136 | bytes 8982528 | tf_op jit(solution)/shard_map/dot_general | solution.py:42
  (4 shorter events, 0.0 us)
Async XLA Ops:
  7.2 82.8 %copy-start = (f32[1,4096]{1,0:T(1,128)S(1)}, f32[1,4096]{1,0:T(1,128)}, u32[]{:S(2)}) copy-start(f32[1,4096]{1,0:T(1,128)} %param.9) | copy-start | bytes 49156
  7.2 69.8 %copy-start.2 = (f32[512]{0:T(512)S(1)}, f32[512]{0:T(512)}, u32[]{:S(2)}) copy-start(f32[512]{0:T(512)} %param.7) | copy-start | bytes 6148
  7.2 69.8 %all-reduce.2.cloned.1.call-start = ((), (), s32[]{:S(2)}) async-start(), calls=%async_computation.1 | async-start | bytes 131072 | tf_op jit(solution)/shard_map/psum | solution.py:16
  44.2 101.3 %reduce-scatter.2.cloned.1.call-start = ((), (), s32[]{:S(2)}) async-start(), calls=%async_computation.2 | async-start | bytes 1179648 | tf_op jit(solution)/shard_map/reduce_scatter | solution.py:27
  76.9 13.0 %copy-start.1 = (bf16[64,512]{1,0:T(8,128)(2,1)S(1)}, bf16[64,512]{1,0:T(8,128)(2,1)}, u32[]{:S(2)}) copy-start(bf16[64,512]{1,0:T(8,128)(2,1)} %all-reduce.2.cloned.1.call-done) | copy-start | bytes 196612
Sparse Core Ops, SparseCore 0:
  44.3 32.6 all-reduce.1
  81.2 64.2 reduce-scatter.1
where the time goes:
time: 231 us
  blocking collectives  110 us (48%)
  waiting for transfers between devices  87 us (38%)
  between operations  15.4 us (7%)
  matrix products  13.2 us (6%)
  other arithmetic  5.29 us (2%)
    reduce_scatter x1, waiting for transfers between devices, local(): lax.psum_scatter(lax.dot_general(w_dec, latents, (((0,), (1,)), ((), ()))...  54.2 us
    psum x1, blocking collectives, local(): loss = lax.psum(square_sum / token_count + penalty_part, ('section', 'mp'))  39.8 us
    all_gather x1, blocking collectives, local(): all_rows = lax.all_gather(activations[0], 'mp', axis=0, tiled=True)  33.2 us
    psum x1, waiting for transfers between devices, local(): lax.psum(partial_value.astype(jnp.bfloat16), 'section').astype(jnp.float32)  32.7 us
    all_gather x1, blocking collectives, local(): lax.all_gather(grad_rec_t, 'mp', axis=0, tiled=True)  31.2 us
    psum x1, blocking collectives, local(): lax.psum(layer_norm.astype(jnp.bfloat16), 'section').astype(jnp.float32)  5.77 us
    dot_general x1, matrix products, local(): lax.dot_general(latents, lax.all_gather(grad_rec_t, 'mp', axis=0, tiled=T...  5.49 us
  transfers between devices with their start and end apart: 2, of which 2 were waited for; matrix products, arithmetic and copies ran while one was open for 2% of the time, Pallas kernels for 0%

commit v1 on v0

--- a/solution.py
+++ b/solution.py
@@ -7,7 +7,12 @@
 
 
 def local(activations, enc_weight, enc_bias, dec_weight, dec_bias):
-    all_rows = lax.all_gather(activations[0], "mp", axis=0, tiled=True)
+    ring = [activations[0]]
+    for hop in range(7):
+        ring.append(lax.ppermute(ring[-1], "mp", [(dev, (dev + 1) % 8) for dev in range(8)]))
+    all_rows = jnp.roll(
+        jnp.concatenate(ring[::-1], axis=0), (lax.axis_index("mp") + 1) * ring[0].shape[0], axis=0
+    )
     token_count = all_rows.shape[0]
     partial_value = jnp.dot(all_rows, enc_weight[0], preferred_element_type=jnp.float32)
     w_dec = dec_weight[:, 0, :]

time: 231 us -> 247 us (1.069)
  waiting for transfers between devices: 87 us -> 131 us
  blocking collectives: 110 us -> 76.8 us
  starting transfers between devices: 0.08 us -> 3.14 us
    ppermute x0 -> x7, waiting for transfers between devices: none -> 47.6 us  [local(): lax.ppermute(ring[-1], 'mp', [(dev, (dev + 1) % 8) for dev in range(8)])]
    all_gather x1 -> x0, blocking collectives: 33.2 us -> none  [local(): all_rows = lax.all_gather(activations[0], 'mp', axis=0, tiled=True)]
    psum x1, waiting for transfers between devices: 32.7 us -> 29.2 us  [local(): lax.psum(partial_value.astype(jnp.bfloat16), 'section').astype(jnp.float32)]
    ppermute x0 -> x7, starting transfers between devices: none -> 3.06 us  [local(): lax.ppermute(ring[-1], 'mp', [(dev, (dev + 1) % 8) for dev in range(8)])]
  transfers between devices with their start and end apart: 2 -> 9, of which waited for: 2 -> 9; matrix products, arithmetic and copies ran while one was open for 2% -> 2% of each run, Pallas kernels for 0% -> 0%
where the time goes in v1:
time: 247 us
  waiting for transfers between devices  131 us (53%)
  blocking collectives  76.8 us (31%)
  between operations  15.5 us (6%)
  matrix products  13.2 us (5%)
  other arithmetic  5.37 us (2%)
  starting transfers between devices  3.14 us (1%)
    reduce_scatter x1, waiting for transfers between devices, local(): lax.psum_scatter(lax.dot_general(w_dec, latents, (((0,), (1,)), ((), ()))...  54.1 us
    ppermute x7, waiting for transfers between devices, local(): lax.ppermute(ring[-1], 'mp', [(dev, (dev + 1) % 8) for dev in range(8)])  47.6 us
    psum x1, blocking collectives, local(): loss = lax.psum(square_sum / token_count + penalty_part, ('section', 'mp'))  39.8 us
    all_gather x1, blocking collectives, local(): lax.all_gather(grad_rec_t, 'mp', axis=0, tiled=True)  31.2 us
    psum x1, waiting for transfers between devices, local(): lax.psum(partial_value.astype(jnp.bfloat16), 'section').astype(jnp.float32)  29.2 us
    psum x1, blocking collectives, local(): lax.psum(layer_norm.astype(jnp.bfloat16), 'section').astype(jnp.float32)  5.77 us
    dot_general x1, matrix products, local(): lax.dot_general(latents, lax.all_gather(grad_rec_t, 'mp', axis=0, tiled=T...  5.49 us
  transfers between devices with their start and end apart: 9, of which 9 were waited for; matrix products, arithmetic and copies ran while one was open for 2% of the time, Pallas kernels for 0%

profile of v1, /device:TPU:0, one launch (start us, length us, event | category | flops | bytes accessed | tf_op | source)
XLA Modules:
  0.0 246.8 jit_solution(4905495257915605706)
XLA Ops:
  7.2 0.0 copy-start
  7.2 0.0 copy-start.2
  7.2 0.0 all-reduce.2.cloned.1.call-start
  7.2 3.0 %collective-permute-start = (bf16[8,4096]{1,0:T(8,128)(2,1)}, bf16[8,4096]{1,0:T(8,128)(2,1)S(1)}, u32[]{:S(2)}, u32[]{:S(2)}) collective-permute-start(bf16[8,4096]{1,0:T(8,128)(2,1)} %bitcast.28), channel_id=1, source_target_pairs={{0,1},{1,2},{2,3},{3,4},{4,5},{5,6},{6,7},{7,0},{8,9},{9,10},{10,1... | collective-permute-start | bytes 196616 | tf_op jit(solution)/shard_map/ppermute | solution.py:12
  10.3 5.5 %collective-permute-done = bf16[8,4096]{1,0:T(8,128)(2,1)S(1)} collective-permute-done((bf16[8,4096]{1,0:T(8,128)(2,1)}, bf16[8,4096]{1,0:T(8,128)(2,1)S(1)}, u32[]{:S(2)}, u32[]{:S(2)}) %collective-permute-start) | collective-permute-done | bytes 65568 | tf_op jit(solution)/shard_map/ppermute | solution.py:12
  15.8 0.0 collective-permute-start.1
  15.8 7.0 %collective-permute-done.1 = bf16[8,4096]{1,0:T(8,128)(2,1)S(1)} collective-permute-done((bf16[8,4096]{1,0:T(8,128)(2,1)S(1)}, bf16[8,4096]{1,0:T(8,128)(2,1)S(1)}, u32[]{:S(2)}, u32[]{:S(2)}) %collective-permute-start.1) | collective-permute-done | bytes 65568 | tf_op jit(solution)/shard_map/ppermute | solution.py:12
  22.7 0.0 collective-permute-start.2
  22.7 7.0 %collective-permute-done.2 = bf16[8,4096]{1,0:T(8,128)(2,1)S(1)} collective-permute-done((bf16[8,4096]{1,0:T(8,128)(2,1)S(1)}, bf16[8,4096]{1,0:T(8,128)(2,1)S(1)}, u32[]{:S(2)}, u32[]{:S(2)}) %collective-permute-start.2) | collective-permute-done | bytes 65568 | tf_op jit(solution)/shard_map/ppermute | solution.py:12
  29.7 0.0 collective-permute-start.3
  29.7 7.0 %collective-permute-done.3 = bf16[8,4096]{1,0:T(8,128)(2,1)S(1)} collective-permute-done((bf16[8,4096]{1,0:T(8,128)(2,1)S(1)}, bf16[8,4096]{1,0:T(8,128)(2,1)S(1)}, u32[]{:S(2)}, u32[]{:S(2)}) %collective-permute-start.3) | collective-permute-done | bytes 65568 | tf_op jit(solution)/shard_map/ppermute | solution.py:12
  36.7 0.0 collective-permute-start.4
  36.7 7.3 %collective-permute-done.4 = bf16[8,4096]{1,0:T(8,128)(2,1)S(1)} collective-permute-done((bf16[8,4096]{1,0:T(8,128)(2,1)S(1)}, bf16[8,4096]{1,0:T(8,128)(2,1)S(1)}, u32[]{:S(2)}, u32[]{:S(2)}) %collective-permute-start.4) | collective-permute-done | bytes 65568 | tf_op jit(solution)/shard_map/ppermute | solution.py:12
  44.0 0.0 collective-permute-start.5
  44.0 7.0 %collective-permute-done.5 = bf16[8,4096]{1,0:T(8,128)(2,1)S(1)} collective-permute-done((bf16[8,4096]{1,0:T(8,128)(2,1)S(1)}, bf16[8,4096]{1,0:T(8,128)(2,1)S(1)}, u32[]{:S(2)}, u32[]{:S(2)}) %collective-permute-start.5) | collective-permute-done | bytes 65568 | tf_op jit(solution)/shard_map/ppermute | solution.py:12
  50.9 0.0 collective-permute-start.6
  50.9 7.0 %collective-permute-done.6 = bf16[8,4096]{1,0:T(8,128)(2,1)S(1)} collective-permute-done((bf16[8,4096]{1,0:T(8,128)(2,1)S(1)}, bf16[8,4096]{1,0:T(8,128)(2,1)S(1)}, u32[]{:S(2)}, u32[]{:S(2)}) %collective-permute-start.6) | collective-permute-done | bytes 65568 | tf_op jit(solution)/shard_map/ppermute | solution.py:12
  58.0 0.8 constant_dynamic-update-slice_fusion.8
  58.9 0.8 constant_dynamic-update-slice_fusion
  59.8 3.7 %fusion.7 = bf16[64,512]{1,0:T(8,128)(2,1)} fusion(bf16[1,4096,512]{2,1,0:T(8,128)(2,1)} %param.6, bf16[128,4096]{1,0:T(8,128)(2,1)S(1)} %constant_dynamic-update-slice_fusion, s32[]{:T(128)S(6)} %select_n.26), kind=kOutput, calls=%fused_computation.10 | convolution fusion | flops 268468224 | bytes 4784132 | tf_op jit(solution)/shard_map/dot_general | solution.py:17
  63.4 0.0 all-reduce.2.cloned.1.call-update
  63.5 0.0 reduce-scatter.2.cloned.1.call-start
  63.5 29.2 %all-reduce.2.cloned.1.call-done = bf16[64,512]{1,0:T(8,128)(2,1)} async-done(((bf16[64,512]{1,0:T(8,128)(2,1)}), bf16[64,512]{1,0:T(8,128)(2,1)}) %all-reduce.2.cloned.1.call-update) | async-done | bytes 65552 | tf_op jit(solution)/shard_map/psum | solution.py:21
  92.7 0.0 copy-done.2
  92.7 0.0 copy-start.1
  92.7 4.1 %convolution_bitcast_fusion = f32[4096,64]{0,1:T(8,128)} fusion(bf16[512,1,4096]{2,0,1:T(8,128)(2,1)} %param.8, bf16[64,512]{1,0:T(8,128)(2,1)} %all-reduce.2.cloned.1.call-done, f32[512]{0:T(512)S(1)} %copy-done.2), kind=kOutput, calls=%fused_computation.6 | convolution fusion | flops 268566528 | bytes 5310464 | tf_op jit(solution)/shard_map/dot_general | solution.py:33
  96.8 0.0 reduce-scatter.2.cloned.1.call-update
  96.8 3.1 %fusion = f32[512]{0:T(512)S(1)} fusion(bf16[512,1,4096]{2,0,1:T(8,128)(2,1)} %param.8), kind=kLoop, calls=%fused_computation.2 | loop fusion | flops 6290944 | bytes 4196352 | tf_op jit(solution)/shard_map/reduce_sum | solution.py:19
  99.9 5.8 %psum.22 = bf16[512]{0:T(512)(128)(2,1)S(1)} all-reduce(bf16[512]{0:T(512)(128)(2,1)S(1)} %sqrt_convert_fusion), channel_id=1, replica_groups=mesh['section'=4,'mp'=8] {'section'}, use_global_device_ids=true, to_apply=%region_4.5 | all-reduce | flops 512 | bytes 2048 | tf_op jit(solution)/shard_map/psum | solution.py:22
  105.7 0.0 copy-done
  105.7 0.0 copy-done.1
  105.7 0.6 convert_reduce_fusion
  107.0 54.1 %reduce-scatter.2.cloned.1.call-done = f32[512,64]{0,1:T(8,128)} async-done(((f32[4096,64]{0,1:T(8,128)}), f32[512,64]{0,1:T(8,128)}) %reduce-scatter.2.cloned.1.call-update) | async-done | bytes 131088 | tf_op jit(solution)/shard_map/reduce_scatter | solution.py:32
  161.1 1.6 multiply_reduce_fusion.1
  163.4 39.8 %psum.23 = f32[]{:T(128)} all-reduce(f32[]{:T(128)S(6)} %add.72), channel_id=1, replica_groups=mesh['section'=4,'mp'=8] {'section','mp'}, use_global_device_ids=true, to_apply=%region_6.7 | all-reduce | flops 1 | bytes 8 | tf_op jit(solution)/shard_map/psum | solution.py:56
  203.3 31.2 %all_gather.3 = bf16[4096,64]{0,1:T(8,128)(2,1)S(1)} all-gather(bf16[512,64]{0,1:T(8,128)(2,1)S(1)} %get-tuple-element.7), channel_id=1, replica_groups=mesh['section'=4,'mp'=8] {'mp'}, dimensions={0}, use_global_device_ids=true | all-gather | bytes 589824 | tf_op jit(solution)/shard_map/all_gather | solution.py:49
  234.5 5.5 %fusion.3 = bf16[512,1,4096]{2,0,1:T(8,128)(2,1)} fusion(bf16[4096,64]{0,1:T(8,128)(2,1)S(1)} %all_gather.3, bf16[512,1,4096]{2,0,1:T(8,128)(2,1)} %param.8, f32[512]{0:T(512)S(1)} %rsqrt_multiply_fusion, bf16[64,512]{1,0:T(8,128)(2,1)S(1)} %copy-done.1, f32[512]{0:T(512)S(1)} %copy-done.2), kind=kOutput, calls=%fused_computation.5 | convolution fusion | flops 276955136 | bytes 8982528 | tf_op jit(solution)/shard_map/dot_general | solution.py:47
  (18 shorter events, 0.1 us)
Async XLA Ops:
  7.2 98.5 %copy-start = (f32[1,4096]{1,0:T(1,128)S(1)}, f32[1,4096]{1,0:T(1,128)}, u32[]{:S(2)}) copy-start(f32[1,4096]{1,0:T(1,128)} %param.9) | copy-start | bytes 49156
  7.2 85.5 %copy-start.2 = (f32[512]{0:T(512)S(1)}, f32[512]{0:T(512)}, u32[]{:S(2)}) copy-start(f32[512]{0:T(512)} %param.7) | copy-start | bytes 6148
  7.2 85.5 %all-reduce.2.cloned.1.call-start = ((), (), s32[]{:S(2)}) async-start(), calls=%async_computation.1 | async-start | bytes 131072 | tf_op jit(solution)/shard_map/psum | solution.py:21
  7.2 8.5 %collective-permute-start = (bf16[8,4096]{1,0:T(8,128)(2,1)}, bf16[8,4096]{1,0:T(8,128)(2,1)S(1)}, u32[]{:S(2)}, u32[]{:S(2)}) collective-permute-start(bf16[8,4096]{1,0:T(8,128)(2,1)} %bitcast.28), channel_id=1, source_target_pairs={{0,1},{1,2},{2,3},{3,4},{4,5},{5,6},{6,7},{7,0},{8,9},{9,10},{10,1... | collective-permute-start | bytes 196616 | tf_op jit(solution)/shard_map/ppermute | solution.py:12
  15.8 7.0 %collective-permute-start.1 = (bf16[8,4096]{1,0:T(8,128)(2,1)S(1)}, bf16[8,4096]{1,0:T(8,128)(2,1)S(1)}, u32[]{:S(2)}, u32[]{:S(2)}) collective-permute-start(bf16[8,4096]{1,0:T(8,128)(2,1)S(1)} %collective-permute-done), channel_id=1, source_target_pairs={{0,1},{1,2},{2,3},{3,4},{4,5},{5,6},{6,7},{7,0},{8,9},{9,10},{10,1... | collective-permute-start | bytes 196616 | tf_op jit(solution)/shard_map/ppermute | solution.py:12
  22.7 7.0 %collective-permute-start.2 = (bf16[8,4096]{1,0:T(8,128)(2,1)S(1)}, bf16[8,4096]{1,0:T(8,128)(2,1)S(1)}, u32[]{:S(2)}, u32[]{:S(2)}) collective-permute-start(bf16[8,4096]{1,0:T(8,128)(2,1)S(1)} %collective-permute-done.1), channel_id=1, source_target_pairs={{0,1},{1,2},{2,3},{3,4},{4,5},{5,6},{6,7},{7,0},{8,9},{9,10},{10,1... | collective-permute-start | bytes 196616 | tf_op jit(solution)/shard_map/ppermute | solution.py:12
  29.7 7.0 %collective-permute-start.3 = (bf16[8,4096]{1,0:T(8,128)(2,1)S(1)}, bf16[8,4096]{1,0:T(8,128)(2,1)S(1)}, u32[]{:S(2)}, u32[]{:S(2)}) collective-permute-start(bf16[8,4096]{1,0:T(8,128)(2,1)S(1)} %collective-permute-done.2), channel_id=1, source_target_pairs={{0,1},{1,2},{2,3},{3,4},{4,5},{5,6},{6,7},{7,0},{8,9},{9,10},{10,1... | collective-permute-start | bytes 196616 | tf_op jit(solution)/shard_map/ppermute | solution.py:12
  36.7 7.3 %collective-permute-start.4 = (bf16[8,4096]{1,0:T(8,128)(2,1)S(1)}, bf16[8,4096]{1,0:T(8,128)(2,1)S(1)}, u32[]{:S(2)}, u32[]{:S(2)}) collective-permute-start(bf16[8,4096]{1,0:T(8,128)(2,1)S(1)} %collective-permute-done.3), channel_id=1, source_target_pairs={{0,1},{1,2},{2,3},{3,4},{4,5},{5,6},{6,7},{7,0},{8,9},{9,10},{10,1... | collective-permute-start | bytes 196616 | tf_op jit(solution)/shard_map/ppermute | solution.py:12
  44.0 7.0 %collective-permute-start.5 = (bf16[8,4096]{1,0:T(8,128)(2,1)S(1)}, bf16[8,4096]{1,0:T(8,128)(2,1)S(1)}, u32[]{:S(2)}, u32[]{:S(2)}) collective-permute-start(bf16[8,4096]{1,0:T(8,128)(2,1)S(1)} %collective-permute-done.4), channel_id=1, source_target_pairs={{0,1},{1,2},{2,3},{3,4},{4,5},{5,6},{6,7},{7,0},{8,9},{9,10},{10,1... | collective-permute-start | bytes 196616 | tf_op jit(solution)/shard_map/ppermute | solution.py:12
  50.9 7.0 %collective-permute-start.6 = (bf16[8,4096]{1,0:T(8,128)(2,1)S(1)}, bf16[8,4096]{1,0:T(8,128)(2,1)S(1)}, u32[]{:S(2)}, u32[]{:S(2)}) collective-permute-start(bf16[8,4096]{1,0:T(8,128)(2,1)S(1)} %collective-permute-done.5), channel_id=1, source_target_pairs={{0,1},{1,2},{2,3},{3,4},{4,5},{5,6},{6,7},{7,0},{8,9},{9,10},{10,1... | collective-permute-start | bytes 196616 | tf_op jit(solution)/shard_map/ppermute | solution.py:12
  63.5 97.7 %reduce-scatter.2.cloned.1.call-start = ((), (), s32[]{:S(2)}) async-start(), calls=%async_computation.2 | async-start | bytes 1179648 | tf_op jit(solution)/shard_map/reduce_scatter | solution.py:32
  92.7 13.0 %copy-start.1 = (bf16[64,512]{1,0:T(8,128)(2,1)S(1)}, bf16[64,512]{1,0:T(8,128)(2,1)}, u32[]{:S(2)}) copy-start(bf16[64,512]{1,0:T(8,128)(2,1)} %all-reduce.2.cloned.1.call-done) | copy-start | bytes 196612
Sparse Core Ops, SparseCore 0:
  63.6 29.0 all-reduce.1
  96.9 64.1 reduce-scatter.1
